TPU v7x, 256 devices: a whole 4x4x8 slice. The times are simulated.
256 devices in a mesh: grp: 16 (over z_lo, x, core), mem: 16 (over y, z_hi).
Axes of the slice: x: 4, y: 4, z: 8 (z_hi: 4, z_lo: 2; z = z_hi * 2 + z_lo), core: 2. Of those that a mesh axis runs over, the one named last changes fastest.
Arguments:
- rhs: float32 [384, 896, 384], P('grp', 'mem'), may hold values from -6 to 6
- conductivity: float32 [384, 896], P('grp', 'mem'), may hold values from 0.2 to 5
- local_inverse: bfloat16 [524288, 2048], P(('grp', 'mem')), may hold values from -0.125 to 0.125
- coarse_basis: float32 [384, 896, 16], P('grp', 'mem'), may hold values from -0.5 to 0.5
- coarse_inverse: float32 [4096, 4096], P(('grp', 'mem')), may hold values from -3 to 8, as said below
Outputs:
- solution: float32 [384, 896, 384], P('grp', 'mem')
Inputs may be any that keep to these rules, and one draw needn't show every extreme that they name: coarse_inverse is symmetric up to rounding, with a positive diagonal.
All inputs are finite; a program needn't handle non-finite values.
Results may differ from a plain program's by a relative error of at most 0.0005.
Values may be sent and summed in bfloat16 or wider, within the bound.
A program may use at most 128 MiB of HBM per device.

v0:
```python
import jax
import jax.numpy as jnp
from jax import lax
from jax.sharding import PartitionSpec as P

OV = 4
ITERS = 2


def padded(block, sides, width):
    for axis, dim in sides:
        count = lax.axis_size(axis)
        forward = [(i, i + 1) for i in range(count - 1)]
        backward = [(target, source) for source, target in forward]
        low = lax.ppermute(
            lax.slice_in_dim(block, block.shape[dim] - width, None, axis=dim), axis, forward
        )
        high = lax.ppermute(lax.slice_in_dim(block, 0, width, axis=dim), axis, backward)
        block = jnp.concatenate([low, block, high], axis=dim)
    return block


def apply_operator(field_pad, conduct_pad):
    center = field_pad[1:-1, 1:-1]
    conduct_mid = conduct_pad[1:-1, 1:-1]
    neighbour_fields = (
        field_pad[2:, 1:-1],
        field_pad[:-2, 1:-1],
        field_pad[1:-1, 2:],
        field_pad[1:-1, :-2],
    )
    neighbour_conduct = (
        conduct_pad[2:, 1:-1],
        conduct_pad[:-2, 1:-1],
        conduct_pad[1:-1, 2:],
        conduct_pad[1:-1, :-2],
    )
    summed = jnp.zeros(center.shape, jnp.float32)
    for other_field, other_conduct in zip(neighbour_fields, neighbour_conduct):
        face = 0.5 * (conduct_mid + other_conduct)
        summed = summed + face[:, :, None] * (center - other_field)
    return summed


def on_device(rhs, conductivity, local_inverse, coarse_basis, coarse_inverse):
    own_x, own_y, columns = rhs.shape
    modes = coarse_basis.shape[2]
    span_x = own_x + 2 * OV
    span_y = own_y + 2 * OV
    owned_inverse = local_inverse.reshape(span_x, span_y, span_x * span_y)[
        OV : OV + own_x, OV : OV + own_y
    ]
    owned_inverse = owned_inverse.reshape(own_x * own_y, span_x * span_y)
    basis_flat = coarse_basis.reshape(own_x * own_y, modes)
    conduct_pad = padded(conductivity, (("grp", 0), ("mem", 1)), 1)
    solution = jnp.zeros(rhs.shape, jnp.float32)
    for sweep in range(ITERS):
        solution_pad = padded(solution, (("grp", 0), ("mem", 1)), 1)
        residual = rhs - apply_operator(solution_pad, conduct_pad)
        rounded = residual.astype(jnp.bfloat16)
        extended = padded(rounded, (("grp", 0), ("mem", 1)), OV)
        flat_rows = extended.reshape(span_x * span_y, columns)
        fine_part = jnp.dot(owned_inverse, flat_rows, preferred_element_type=jnp.float32).reshape(
            own_x, own_y, columns
        )
        restricted = lax.dot_general(
            basis_flat,
            residual.reshape(own_x * own_y, columns),
            (((0,), (0,)), ((), ())),
            precision=lax.Precision.HIGHEST,
            preferred_element_type=jnp.float32,
        )
        group_block = lax.all_gather(restricted, "mem", axis=0, tiled=True)
        lifted = jnp.dot(
            coarse_inverse,
            lax.all_gather(group_block, "grp", axis=0, tiled=True),
            precision=lax.Precision.HIGHEST,
            preferred_element_type=jnp.float32,
        )
        coarse_part = jnp.dot(
            basis_flat, lifted, precision=lax.Precision.HIGHEST, preferred_element_type=jnp.float32
        ).reshape(own_x, own_y, columns)
        solution = solution + fine_part + coarse_part
    return solution


def solution(mesh):
    placed = (
        P("grp", "mem", None),
        P("grp", "mem"),
        P(("grp", "mem"), None),
        P("grp", "mem", None),
        P(("grp", "mem"), None),
    )
    return jax.shard_map(
        on_device, mesh=mesh, in_specs=placed, out_specs=P("grp", "mem", None), check_vma=False
    )
```

profile of v0, /device:TPU:65, one launch (start us, length us, event | category | flops | bytes accessed | tf_op | source)
XLA Modules:
  0.0 280.6 jit_solution(17195982681964429826)
XLA Ops:
  7.3 3.7 %collective-permute-start.2 = (f32[1,56]{1,0:T(1,128)S(1)}, f32[1,56]{1,0:T(1,128)S(1)}, u32[]{:S(2)}, u32[]{:S(2)}) collective-permute-start(f32[1,56]{1,0:T(1,128)S(1)} %get-tuple-element.29), channel_id=1, source_target_pairs={{0,16},{16,32},{32,48},{48,64},{64,80},{80,96},{96,112},{112,128},... | collective-permute-start | bytes 680 | tf_op jit(solution)/shard_map/ppermute | solution.py:15
  11.0 1.9 collective-permute-start
  12.9 3.6 %collective-permute-start.3 = (f32[1,56,384]{2,1,0:T(8,128)S(1)}, f32[1,56,384]{2,1,0:T(8,128)S(1)}, u32[]{:S(2)}, u32[]{:S(2)}) collective-permute-start(f32[1,56,384]{2,1,0:T(8,128)S(1)} %broadcast.15), channel_id=1, source_target_pairs={{0,16},{16,32},{32,48},{48,64},{64,80},{80,96},{96,112},{112,128},... | collective-permute-start | bytes 258056 | tf_op jit(solution)/shard_map/ppermute | solution.py:15
  16.6 1.9 collective-permute-start.1
  21.2 6.2 %collective-permute-start.6 = (f32[26,1]{1,0:T(8,128)S(1)}, f32[26,1]{1,0:T(8,128)S(1)}, u32[]{:S(2)}, u32[]{:S(2)}) collective-permute-start(f32[26,1]{1,0:T(8,128)S(1)} %get-tuple-element.24), channel_id=1, source_target_pairs={{0,1},{1,2},{2,3},{3,4},{4,5},{5,6},{6,7},{7,8},{8,9},{9,10},{10,1... | collective-permute-start | bytes 320 | tf_op jit(solution)/shard_map/ppermute | solution.py:15
  27.7 1.9 collective-permute-start.5
  29.7 5.5 %collective-permute-start.7 = (f32[26,1,384]{2,1,0:T(1,128)S(1)}, f32[26,1,384]{2,1,0:T(1,128)S(1)}, u32[]{:S(2)}, u32[]{:S(2)}) collective-permute-start(f32[26,1,384]{2,1,0:T(1,128)S(1)} %get-tuple-element.12), channel_id=1, source_target_pairs={{0,1},{1,2},{2,3},{3,4},{4,5},{5,6},{6,7},{7,8},{8,9},{9,10},{10,1... | collective-permute-start | bytes 119816 | tf_op jit(solution)/shard_map/ppermute | solution.py:15
  36.2 3.1 %fusion.34 = (bf16[24,56,384]{2,1,0:T(8,128)(2,1)S(1)}, f32[24,56,384]{2,1,0:T(8,128)S(1)}) fusion(f32[24,56,384]{2,1,0:T(8,128)S(1)} %copy-done.1, f32[24,56,384]{2,1,0:T(8,128)S(1)} %broadcast_in_dim.2, f32[1,56,384]{2,1,0:T(8,128)S(1)} %collective-permute-done.1, f32[1,56,384]{2,1,0:T(8,128)S(1)} %collective-permute-done.3, ...), kind=kLoop, calls=%fused_computation.78 | loop fusion | flops 9805824 | bytes 7498752 | tf_op jit(solution)/shard_map/convert_element_type | solution.py:60
  40.6 40.6 %all_gather.12 = f32[256,384]{1,0:T(8,128)} all-gather(f32[16,384]{1,0:T(8,128)S(1)} %convolution_bitcast_fusion.1), channel_id=1, replica_groups=mesh['grp'=16,'mem'=16] {'mem'}, dimensions={0}, use_global_device_ids=true | all-gather | bytes 417792 | tf_op jit(solution)/shard_map/all_gather | solution.py:73
  81.3 11.7 %collective-permute-start.8 = (bf16[4,56,384]{2,1,0:T(8,128)(2,1)S(1)}, bf16[4,56,384]{2,1,0:T(8,128)(2,1)S(1)}, u32[]{:S(2)}, u32[]{:S(2)}) collective-permute-start(bf16[4,56,384]{2,1,0:T(8,128)(2,1)S(1)} %get-tuple-element.21), channel_id=1, source_target_pairs={{0,16},{16,32},{32,48},{48,64},{64,80},{80,96},{96,112},{112,128},... | collective-permute-start | bytes 516104 | tf_op jit(solution)/shard_map/ppermute | solution.py:15
  93.0 1.9 collective-permute-start.9
  95.3 4.4 %collective-permute-done.9 = bf16[4,56,384]{2,1,0:T(8,128)(2,1)S(1)} collective-permute-done((bf16[4,56,384]{2,1,0:T(8,128)(2,1)S(1)}, bf16[4,56,384]{2,1,0:T(8,128)(2,1)S(1)}, u32[]{:S(2)}, u32[]{:S(2)}) %collective-permute-start.9) | collective-permute-done | bytes 172064 | tf_op jit(solution)/shard_map/ppermute | solution.py:18
  99.8 3.2 %collective-permute-start.10 = (bf16[32,4,384]{2,1,0:T(4,128)(2,1)S(1)}, bf16[32,4,384]{2,1,0:T(4,128)(2,1)S(1)}, u32[]{:S(2)}, u32[]{:S(2)}) collective-permute-start(bf16[32,4,384]{2,1,0:T(4,128)(2,1)S(1)} %get-tuple-element.17), channel_id=1, source_target_pairs={{0,1},{1,2},{2,3},{3,4},{4,5},{5,6},{6,7},{7,8},{8,9},{9,10},{10,1... | collective-permute-start | bytes 294920 | tf_op jit(solution)/shard_map/ppermute | solution.py:15
  103.0 6.4 %collective-permute-start.11 = (bf16[32,4,384]{2,1,0:T(4,128)(2,1)S(1)}, bf16[32,4,384]{2,1,0:T(4,128)(2,1)S(1)}, u32[]{:S(2)}, u32[]{:S(2)}) collective-permute-start(bf16[32,4,384]{2,1,0:T(4,128)(2,1)S(1)} %get-tuple-element.18), channel_id=1, source_target_pairs={{1,0},{2,1},{3,2},{4,3},{5,4},{6,5},{7,6},{8,7},{9,8},{10,9},{11,1... | collective-permute-start | bytes 294920 | tf_op jit(solution)/shard_map/ppermute | solution.py:18
  109.6 8.3 %slice.148 = bf16[24,56,2048]{2,1,0:T(8,128)(2,1)} slice(bf16[32,64,2048]{2,1,0:T(8,128)(2,1)} %bitcast.50), slice={[4:28], [4:60], [0:2048]} | slice | bytes 11010048 | tf_op jit(solution)/shard_map/slice | solution.py:50
  118.0 2.1 pad_maximum_fusion.14
  120.0 19.4 %all-gather.3.cloned.1.call-done = f32[4096,384]{1,0:T(8,128)} async-done(((f32[256,384]{1,0:T(8,128)}), f32[4096,384]{1,0:T(8,128)}) %all-gather.3.cloned.1.call-update) | async-done | bytes 6291472 | tf_op jit(solution)/shard_map/all_gather | solution.py:76
  139.4 5.5 %fusion.40 = f32[384,16]{0,1:T(8,128)S(1)} fusion(f32[4096,384]{1,0:T(8,128)} %all-gather.3.cloned.1.call-done, f32[16,4096]{1,0:T(8,128)S(1)} %copy-done), kind=kOutput, calls=%fused_computation.83 | convolution fusion | flops 301989888 | bytes 6578176 | tf_op jit(solution)/shard_map/dot_general | solution.py:74
  146.9 3.1 %convolution_add_fusion = f32[384,1344]{0,1:T(8,128)S(1)} fusion(f32[384,1344]{0,1:T(8,128)S(1)} %fusion.41, bf16[1344,2048]{1,0:T(8,128)(2,1)S(1)} %bitcast.49, bf16[2048,384]{1,0:T(8,128)(2,1)S(1)} %bitcast.52), kind=kOutput, calls=%fused_computation | convolution fusion | flops 2114445312 | bytes 11206656 | tf_op jit(solution)/shard_map/dot_general | solution.py:63
  150.1 2.4 collective-permute-start.13
  152.6 2.0 collective-permute-start.12
  154.6 3.8 %collective-permute-done.12 = f32[1,56,384]{2,1,0:T(8,128)S(1)} collective-permute-done((f32[1,56,384]{2,1,0:T(8,128)S(1)}, f32[1,56,384]{2,1,0:T(8,128)S(1)}, u32[]{:S(2)}, u32[]{:S(2)}) %collective-permute-start.12) | collective-permute-done | bytes 86048 | tf_op jit(solution)/shard_map/ppermute | solution.py:18
  160.3 5.7 %collective-permute-start.15 = (f32[26,1,384]{2,1,0:T(1,128)S(1)}, f32[26,1,384]{2,1,0:T(1,128)S(1)}, u32[]{:S(2)}, u32[]{:S(2)}) collective-permute-start(f32[26,1,384]{2,1,0:T(1,128)S(1)} %get-tuple-element.10), channel_id=1, source_target_pairs={{0,1},{1,2},{2,3},{3,4},{4,5},{5,6},{6,7},{7,8},{8,9},{9,10},{10,1... | collective-permute-start | bytes 119816 | tf_op jit(solution)/shard_map/ppermute | solution.py:15
  167.1 3.4 %fusion.32 = (bf16[24,56,384]{2,1,0:T(8,128)(2,1)S(1)}, f32[24,56,384]{2,1,0:T(8,128)S(1)}) fusion(f32[24,56,384]{2,1,0:T(8,128)S(1)} %copy-done.2, f32[24,56,384]{2,1,0:T(8,128)S(1)} %bitcast.45, f32[1,56,384]{2,1,0:T(8,128)S(1)} %collective-permute-done.12, f32[1,56,384]{2,1,0:T(8,128)S(1)} %collective-permute-done.13, ...), kind=kLoop, calls=%fused_computation.77 | loop fusion | flops 10838016 | bytes 7498752 | tf_op jit(solution)/shard_map/convert_element_type | solution.py:60
  171.8 38.1 %all_gather.14 = f32[256,384]{1,0:T(8,128)} all-gather(f32[16,384]{1,0:T(8,128)S(1)} %convolution_bitcast_fusion), channel_id=1, replica_groups=mesh['grp'=16,'mem'=16] {'mem'}, dimensions={0}, use_global_device_ids=true | all-gather | bytes 417792 | tf_op jit(solution)/shard_map/all_gather | solution.py:73
  210.0 11.0 %collective-permute-start.16 = (bf16[4,56,384]{2,1,0:T(8,128)(2,1)S(1)}, bf16[4,56,384]{2,1,0:T(8,128)(2,1)S(1)}, u32[]{:S(2)}, u32[]{:S(2)}) collective-permute-start(bf16[4,56,384]{2,1,0:T(8,128)(2,1)S(1)} %get-tuple-element.19), channel_id=1, source_target_pairs={{0,16},{16,32},{32,48},{48,64},{64,80},{80,96},{96,112},{112,128},... | collective-permute-start | bytes 516104 | tf_op jit(solution)/shard_map/ppermute | solution.py:15
  223.4 5.9 %collective-permute-done.17 = bf16[4,56,384]{2,1,0:T(8,128)(2,1)S(1)} collective-permute-done((bf16[4,56,384]{2,1,0:T(8,128)(2,1)S(1)}, bf16[4,56,384]{2,1,0:T(8,128)(2,1)S(1)}, u32[]{:S(2)}, u32[]{:S(2)}) %collective-permute-start.17) | collective-permute-done | bytes 172064 | tf_op jit(solution)/shard_map/ppermute | solution.py:18
  231.3 6.0 %collective-permute-start.19 = (bf16[32,4,384]{2,1,0:T(4,128)(2,1)S(1)}, bf16[32,4,384]{2,1,0:T(4,128)(2,1)S(1)}, u32[]{:S(2)}, u32[]{:S(2)}) collective-permute-start(bf16[32,4,384]{2,1,0:T(4,128)(2,1)S(1)} %get-tuple-element.16), channel_id=1, source_target_pairs={{1,0},{2,1},{3,2},{4,3},{5,4},{6,5},{7,6},{8,7},{9,8},{10,9},{11,1... | collective-permute-start | bytes 294920 | tf_op jit(solution)/shard_map/ppermute | solution.py:18
  237.3 3.1 %collective-permute-done.18 = bf16[32,4,384]{2,1,0:T(4,128)(2,1)S(1)} collective-permute-done((bf16[32,4,384]{2,1,0:T(4,128)(2,1)S(1)}, bf16[32,4,384]{2,1,0:T(4,128)(2,1)S(1)}, u32[]{:S(2)}, u32[]{:S(2)}) %collective-permute-start.18) | collective-permute-done | bytes 98336 | tf_op jit(solution)/shard_map/ppermute | solution.py:15
  241.4 7.0 %fusion.44 = f32[384,1344]{0,1:T(8,128)} fusion(bf16[1344,2048]{1,0:T(8,128)(2,1)} %bitcast.48, bf16[2048,384]{1,0:T(8,128)(2,1)S(1)} %bitcast.53), kind=kOutput, calls=%fused_computation.87 | convolution fusion | flops 2113929216 | bytes 9142272 | tf_op jit(solution)/shard_map/dot_general | solution.py:63
  248.3 16.5 %all-gather.5.cloned.1.call-done = f32[4096,384]{1,0:T(8,128)} async-done(((f32[256,384]{1,0:T(8,128)}), f32[4096,384]{1,0:T(8,128)}) %all-gather.5.cloned.1.call-update) | async-done | bytes 6291472 | tf_op jit(solution)/shard_map/all_gather | solution.py:76
  264.9 5.4 %fusion.42 = f32[384,16]{0,1:T(8,128)S(1)} fusion(f32[4096,384]{1,0:T(8,128)} %all-gather.5.cloned.1.call-done, f32[16,4096]{1,0:T(8,128)S(1)} %copy-done), kind=kOutput, calls=%fused_computation.85 | convolution fusion | flops 301989888 | bytes 6578176 | tf_op jit(solution)/shard_map/dot_general | solution.py:74
  (81 shorter events, 21.6 us)
Async XLA Ops:
  6.5 132.9 %copy-start = (f32[16,4096]{1,0:T(8,128)S(1)}, f32[16,4096]{1,0:T(8,128)}, u32[]{:S(2)}) copy-start(f32[16,4096]{1,0:T(8,128)} %param.9) | copy-start | bytes 786436
  6.5 132.9 %all-gather.3.cloned.1.call-start = ((), (), s32[]{:S(2)}) async-start(), calls=%async_computation | async-start | bytes 6684672 | tf_op jit(solution)/shard_map/all_gather | solution.py:76
  7.3 11.2 %collective-permute-start.2 = (f32[1,56]{1,0:T(1,128)S(1)}, f32[1,56]{1,0:T(1,128)S(1)}, u32[]{:S(2)}, u32[]{:S(2)}) collective-permute-start(f32[1,56]{1,0:T(1,128)S(1)} %get-tuple-element.29), channel_id=1, source_target_pairs={{0,16},{16,32},{32,48},{48,64},{64,80},{80,96},{96,112},{112,128},... | collective-permute-start | bytes 680 | tf_op jit(solution)/shard_map/ppermute | solution.py:15
  11.0 7.5 %collective-permute-start = (f32[1,56]{1,0:T(1,128)S(1)}, f32[1,56]{1,0:T(1,128)S(1)}, u32[]{:S(2)}, u32[]{:S(2)}) collective-permute-start(f32[1,56]{1,0:T(1,128)S(1)} %get-tuple-element.30), channel_id=1, source_target_pairs={{16,0},{32,16},{48,32},{64,48},{80,64},{96,80},{112,96},{128,112},... | collective-permute-start | bytes 680 | tf_op jit(solution)/shard_map/ppermute | solution.py:18
  12.9 14.6 %collective-permute-start.3 = (f32[1,56,384]{2,1,0:T(8,128)S(1)}, f32[1,56,384]{2,1,0:T(8,128)S(1)}, u32[]{:S(2)}, u32[]{:S(2)}) collective-permute-start(f32[1,56,384]{2,1,0:T(8,128)S(1)} %broadcast.15), channel_id=1, source_target_pairs={{0,16},{16,32},{32,48},{48,64},{64,80},{80,96},{96,112},{112,128},... | collective-permute-start | bytes 258056 | tf_op jit(solution)/shard_map/ppermute | solution.py:15
  16.6 10.9 %collective-permute-start.1 = (f32[1,56,384]{2,1,0:T(8,128)S(1)}, f32[1,56,384]{2,1,0:T(8,128)S(1)}, u32[]{:S(2)}, u32[]{:S(2)}) collective-permute-start(f32[1,56,384]{2,1,0:T(8,128)S(1)} %broadcast.15), channel_id=1, source_target_pairs={{16,0},{32,16},{48,32},{64,48},{80,64},{96,80},{112,96},{128,112},... | collective-permute-start | bytes 258056 | tf_op jit(solution)/shard_map/ppermute | solution.py:18
  19.3 15.8 %collective-permute-start.4 = (f32[26,1]{1,0:T(8,128)S(1)}, f32[26,1]{1,0:T(8,128)S(1)}, u32[]{:S(2)}, u32[]{:S(2)}) collective-permute-start(f32[26,1]{1,0:T(8,128)S(1)} %get-tuple-element.23), channel_id=1, source_target_pairs={{1,0},{2,1},{3,2},{4,3},{5,4},{6,5},{7,6},{8,7},{9,8},{10,9},{11,1... | collective-permute-start | bytes 320 | tf_op jit(solution)/shard_map/ppermute | solution.py:18
  21.2 13.9 %copy-start.17 = (f32[24,56]{1,0:T(8,128)S(1)}, f32[24,56]{1,0:T(8,128)}, u32[]{:S(2)}) copy-start(f32[24,56]{1,0:T(8,128)} %param.6) | copy-start | bytes 16132
  21.2 15.0 %copy-start.1 = (f32[24,56,384]{2,1,0:T(8,128)S(1)}, f32[24,56,384]{2,1,0:T(8,128)}, u32[]{:S(2)}) copy-start(f32[24,56,384]{2,1,0:T(8,128)} %param.5) | copy-start | bytes 6193156
  21.2 13.9 %collective-permute-start.6 = (f32[26,1]{1,0:T(8,128)S(1)}, f32[26,1]{1,0:T(8,128)S(1)}, u32[]{:S(2)}, u32[]{:S(2)}) collective-permute-start(f32[26,1]{1,0:T(8,128)S(1)} %get-tuple-element.24), channel_id=1, source_target_pairs={{0,1},{1,2},{2,3},{3,4},{4,5},{5,6},{6,7},{7,8},{8,9},{9,10},{10,1... | collective-permute-start | bytes 320 | tf_op jit(solution)/shard_map/ppermute | solution.py:15
  27.7 7.6 %collective-permute-start.5 = (f32[26,1,384]{2,1,0:T(1,128)S(1)}, f32[26,1,384]{2,1,0:T(1,128)S(1)}, u32[]{:S(2)}, u32[]{:S(2)}) collective-permute-start(f32[26,1,384]{2,1,0:T(1,128)S(1)} %get-tuple-element.11), channel_id=1, source_target_pairs={{1,0},{2,1},{3,2},{4,3},{5,4},{6,5},{7,6},{8,7},{9,8},{10,9},{11,1... | collective-permute-start | bytes 119816 | tf_op jit(solution)/shard_map/ppermute | solution.py:18
  29.7 6.5 %collective-permute-start.7 = (f32[26,1,384]{2,1,0:T(1,128)S(1)}, f32[26,1,384]{2,1,0:T(1,128)S(1)}, u32[]{:S(2)}, u32[]{:S(2)}) collective-permute-start(f32[26,1,384]{2,1,0:T(1,128)S(1)} %get-tuple-element.12), channel_id=1, source_target_pairs={{0,1},{1,2},{2,3},{3,4},{4,5},{5,6},{6,7},{7,8},{8,9},{9,10},{10,1... | collective-permute-start | bytes 119816 | tf_op jit(solution)/shard_map/ppermute | solution.py:15
  81.3 183.6 %all-gather.5.cloned.1.call-start = ((), (), s32[]{:S(2)}) async-start(), calls=%async_computation.1 | async-start | bytes 6684672 | tf_op jit(solution)/shard_map/all_gather | solution.py:76
  81.3 14.0 %collective-permute-start.8 = (bf16[4,56,384]{2,1,0:T(8,128)(2,1)S(1)}, bf16[4,56,384]{2,1,0:T(8,128)(2,1)S(1)}, u32[]{:S(2)}, u32[]{:S(2)}) collective-permute-start(bf16[4,56,384]{2,1,0:T(8,128)(2,1)S(1)} %get-tuple-element.21), channel_id=1, source_target_pairs={{0,16},{16,32},{32,48},{48,64},{64,80},{80,96},{96,112},{112,128},... | collective-permute-start | bytes 516104 | tf_op jit(solution)/shard_map/ppermute | solution.py:15
  93.0 6.7 %collective-permute-start.9 = (bf16[4,56,384]{2,1,0:T(8,128)(2,1)S(1)}, bf16[4,56,384]{2,1,0:T(8,128)(2,1)S(1)}, u32[]{:S(2)}, u32[]{:S(2)}) collective-permute-start(bf16[4,56,384]{2,1,0:T(8,128)(2,1)S(1)} %get-tuple-element.22), channel_id=1, source_target_pairs={{16,0},{32,16},{48,32},{64,48},{80,64},{96,80},{112,96},{128,112},... | collective-permute-start | bytes 516104 | tf_op jit(solution)/shard_map/ppermute | solution.py:18
  99.8 18.1 %collective-permute-start.10 = (bf16[32,4,384]{2,1,0:T(4,128)(2,1)S(1)}, bf16[32,4,384]{2,1,0:T(4,128)(2,1)S(1)}, u32[]{:S(2)}, u32[]{:S(2)}) collective-permute-start(bf16[32,4,384]{2,1,0:T(4,128)(2,1)S(1)} %get-tuple-element.17), channel_id=1, source_target_pairs={{0,1},{1,2},{2,3},{3,4},{4,5},{5,6},{6,7},{7,8},{8,9},{9,10},{10,1... | collective-permute-start | bytes 294920 | tf_op jit(solution)/shard_map/ppermute | solution.py:15
  103.0 14.9 %collective-permute-start.11 = (bf16[32,4,384]{2,1,0:T(4,128)(2,1)S(1)}, bf16[32,4,384]{2,1,0:T(4,128)(2,1)S(1)}, u32[]{:S(2)}, u32[]{:S(2)}) collective-permute-start(bf16[32,4,384]{2,1,0:T(4,128)(2,1)S(1)} %get-tuple-element.18), channel_id=1, source_target_pairs={{1,0},{2,1},{3,2},{4,3},{5,4},{6,5},{7,6},{8,7},{9,8},{10,9},{11,1... | collective-permute-start | bytes 294920 | tf_op jit(solution)/shard_map/ppermute | solution.py:18
  109.6 35.4 %copy-start.7 = (f32[1344,16]{0,1:T(8,128)}, f32[1344,16]{0,1:T(8,128)S(1)}, u32[]{:S(2)}) copy-start(f32[1344,16]{0,1:T(8,128)S(1)} %reshape.35) | copy-start | bytes 258052
  150.0 17.1 %copy-start.2 = (f32[24,56,384]{2,1,0:T(8,128)S(1)}, f32[24,56,384]{2,1,0:T(8,128)}, u32[]{:S(2)}) copy-start(f32[24,56,384]{2,1,0:T(8,128)} %param.5) | copy-start | bytes 6193156
  150.1 17.1 %copy-start.10 = (f32[24,56]{1,0:T(8,128)S(1)}, f32[24,56]{1,0:T(8,128)}, u32[]{:S(2)}) copy-start(f32[24,56]{1,0:T(8,128)} %copy-done.9) | copy-start | bytes 16132
  150.1 17.1 %copy-start.12 = (f32[24,56]{1,0:T(8,128)S(1)}, f32[24,56]{1,0:T(8,128)}, u32[]{:S(2)}) copy-start(f32[24,56]{1,0:T(8,128)} %copy-done.11) | copy-start | bytes 16132
  150.1 17.0 %copy-start.14 = (f32[24,56]{1,0:T(8,128)S(1)}, f32[24,56]{1,0:T(8,128)}, u32[]{:S(2)}) copy-start(f32[24,56]{1,0:T(8,128)} %copy-done.13) | copy-start | bytes 16132
  150.1 17.0 %copy-start.16 = (f32[24,56]{1,0:T(8,128)S(1)}, f32[24,56]{1,0:T(8,128)}, u32[]{:S(2)}) copy-start(f32[24,56]{1,0:T(8,128)} %copy-done.15) | copy-start | bytes 16132
  150.1 4.5 %collective-permute-start.13 = (f32[1,56,384]{2,1,0:T(8,128)S(1)}, f32[1,56,384]{2,1,0:T(8,128)S(1)}, u32[]{:S(2)}, u32[]{:S(2)}) collective-permute-start(f32[1,56,384]{2,1,0:T(8,128)S(1)} %get-tuple-element.13), channel_id=1, source_target_pairs={{0,16},{16,32},{32,48},{48,64},{64,80},{80,96},{96,112},{112,128},... | collective-permute-start | bytes 258056 | tf_op jit(solution)/shard_map/ppermute | solution.py:15
  152.6 5.8 %collective-permute-start.12 = (f32[1,56,384]{2,1,0:T(8,128)S(1)}, f32[1,56,384]{2,1,0:T(8,128)S(1)}, u32[]{:S(2)}, u32[]{:S(2)}) collective-permute-start(f32[1,56,384]{2,1,0:T(8,128)S(1)} %get-tuple-element.14), channel_id=1, source_target_pairs={{16,0},{32,16},{48,32},{64,48},{80,64},{96,80},{112,96},{128,112},... | collective-permute-start | bytes 258056 | tf_op jit(solution)/shard_map/ppermute | solution.py:18
  158.4 7.6 %collective-permute-start.14 = (f32[26,1,384]{2,1,0:T(1,128)S(1)}, f32[26,1,384]{2,1,0:T(1,128)S(1)}, u32[]{:S(2)}, u32[]{:S(2)}) collective-permute-start(f32[26,1,384]{2,1,0:T(1,128)S(1)} %get-tuple-element.9), channel_id=1, source_target_pairs={{1,0},{2,1},{3,2},{4,3},{5,4},{6,5},{7,6},{8,7},{9,8},{10,9},{11,1... | collective-permute-start | bytes 119816 | tf_op jit(solution)/shard_map/ppermute | solution.py:18
  160.3 6.8 %collective-permute-start.15 = (f32[26,1,384]{2,1,0:T(1,128)S(1)}, f32[26,1,384]{2,1,0:T(1,128)S(1)}, u32[]{:S(2)}, u32[]{:S(2)}) collective-permute-start(f32[26,1,384]{2,1,0:T(1,128)S(1)} %get-tuple-element.10), channel_id=1, source_target_pairs={{0,1},{1,2},{2,3},{3,4},{4,5},{5,6},{6,7},{7,8},{8,9},{9,10},{10,1... | collective-permute-start | bytes 119816 | tf_op jit(solution)/shard_map/ppermute | solution.py:15
  210.0 13.4 %collective-permute-start.16 = (bf16[4,56,384]{2,1,0:T(8,128)(2,1)S(1)}, bf16[4,56,384]{2,1,0:T(8,128)(2,1)S(1)}, u32[]{:S(2)}, u32[]{:S(2)}) collective-permute-start(bf16[4,56,384]{2,1,0:T(8,128)(2,1)S(1)} %get-tuple-element.19), channel_id=1, source_target_pairs={{0,16},{16,32},{32,48},{48,64},{64,80},{80,96},{96,112},{112,128},... | collective-permute-start | bytes 516104 | tf_op jit(solution)/shard_map/ppermute | solution.py:15
  221.1 8.2 %collective-permute-start.17 = (bf16[4,56,384]{2,1,0:T(8,128)(2,1)S(1)}, bf16[4,56,384]{2,1,0:T(8,128)(2,1)S(1)}, u32[]{:S(2)}, u32[]{:S(2)}) collective-permute-start(bf16[4,56,384]{2,1,0:T(8,128)(2,1)S(1)} %get-tuple-element.20), channel_id=1, source_target_pairs={{16,0},{32,16},{48,32},{64,48},{80,64},{96,80},{112,96},{128,112},... | collective-permute-start | bytes 516104 | tf_op jit(solution)/shard_map/ppermute | solution.py:18
  229.4 11.1 %collective-permute-start.18 = (bf16[32,4,384]{2,1,0:T(4,128)(2,1)S(1)}, bf16[32,4,384]{2,1,0:T(4,128)(2,1)S(1)}, u32[]{:S(2)}, u32[]{:S(2)}) collective-permute-start(bf16[32,4,384]{2,1,0:T(4,128)(2,1)S(1)} %get-tuple-element.15), channel_id=1, source_target_pairs={{0,1},{1,2},{2,3},{3,4},{4,5},{5,6},{6,7},{7,8},{8,9},{9,10},{10,1... | collective-permute-start | bytes 294920 | tf_op jit(solution)/shard_map/ppermute | solution.py:15
  231.3 9.2 %collective-permute-start.19 = (bf16[32,4,384]{2,1,0:T(4,128)(2,1)S(1)}, bf16[32,4,384]{2,1,0:T(4,128)(2,1)S(1)}, u32[]{:S(2)}, u32[]{:S(2)}) collective-permute-start(bf16[32,4,384]{2,1,0:T(4,128)(2,1)S(1)} %get-tuple-element.16), channel_id=1, source_target_pairs={{1,0},{2,1},{3,2},{4,3},{5,4},{6,5},{7,6},{8,7},{9,8},{10,9},{11,1... | collective-permute-start | bytes 294920 | tf_op jit(solution)/shard_map/ppermute | solution.py:18
  248.3 21.9 %copy-start.8 = (f32[1344,16]{0,1:T(8,128)S(1)}, f32[1344,16]{0,1:T(8,128)}, u32[]{:S(2)}) copy-start(f32[1344,16]{0,1:T(8,128)} %copy-done.7) | copy-start | bytes 258052
  (8 other events, 30.4 us)
Sparse Core Ops, SparseCore 0:
  81.4 58.0 all-gather.2
  210.1 54.7 all-gather.4
where the time goes:
time: 281 us
  starting transfers between devices  82.9 us (30%)
  blocking collectives  78.8 us (28%)
  waiting for transfers between devices  55.9 us (20%)
  matrix products  27.2 us (10%)
  between operations  14 us (5%)
  other arithmetic  12.2 us (4%)
  local copies, waits for them, and re-layouts  9.66 us (3%)
    all_gather x2, blocking collectives, on_device(): group_block = lax.all_gather(restricted, 'mem', axis=0, tiled=True)  78.8 us
    ppermute x10, starting transfers between devices, padded(): lax.ppermute(lax.slice_in_dim(block, block.shape[dim] - width, None, axis...  54.9 us
    all_gather x2, waiting for transfers between devices, on_device(): lax.all_gather(group_block, 'grp', axis=0, tiled=True)  35.9 us
    ppermute x10, starting transfers between devices, padded(): lax.ppermute(lax.slice_in_dim(block, 0, width, axis=dim), axis, backward)  27.9 us
    ppermute x10, waiting for transfers between devices, padded(): lax.ppermute(lax.slice_in_dim(block, 0, width, axis=dim), axis, backward)  14.1 us
    dot_general x2, matrix products, on_device(): jnp.dot(coarse_inverse, lax.all_gather(group_block, 'grp', axis=0, tiled=...  10.9 us
    dot_general x2, matrix products, on_device(): jnp.dot(owned_inverse, flat_rows, preferred_element_type=jnp.float32)  10.1 us
    slice x1, local copies, waits for them, and re-layouts, on_device(): local_inverse.reshape(span_x, span_y, span_x * span_y)  8.33 us
  transfers between devices with their start and end apart: 22, of which 10 were waited for; matrix products, arithmetic and copies ran while one was open for 7% of the time, Pallas kernels for 0%

commit v1 on v0

--- a/solution.py
+++ b/solution.py
@@ -73,7 +73,9 @@
         group_block = lax.all_gather(restricted, "mem", axis=0, tiled=True)
         lifted = jnp.dot(
             coarse_inverse,
-            lax.all_gather(group_block, "grp", axis=0, tiled=True),
+            jnp.concatenate(
+                lax.all_to_all(jnp.stack([group_block] * lax.axis_size("grp")), "grp", 0, 0), axis=0
+            ),
             precision=lax.Precision.HIGHEST,
             preferred_element_type=jnp.float32,
         )

time: 281 us -> 414 us (1.47); the launches traced: 281 us -> 407 us
  waiting for transfers between devices: 55.9 us -> 161 us
  starting transfers between devices: 82.9 us -> 103 us
  between operations: 14 us -> 0.59 us
  matrix products: 27.2 us -> 40.6 us
  local copies, waits for them, and re-layouts: 9.66 us -> 16.2 us
  blocking collectives: 78.8 us -> 73.5 us
    ppermute x10, waiting for transfers between devices: 5.88 us -> 126 us  [padded(): lax.ppermute(lax.slice_in_dim(block, block.shape[dim] - width, None, axis...]
    all_to_all x0 -> x2, starting transfers between devices: none -> 36.5 us  [on_device(): lax.all_to_all(jnp.stack([group_block] * lax.axis_size('grp')), 'grp', 0, 0)]
    all_gather x2 -> x0, waiting for transfers between devices: 35.9 us -> none  [on_device(): lax.all_gather(group_block, 'grp', axis=0, tiled=True)]
    ppermute x10, waiting for transfers between devices: 14.1 us -> 34.6 us  [padded(): lax.ppermute(lax.slice_in_dim(block, 0, width, axis=dim), axis, backward)]
    ppermute x10, starting transfers between devices: 54.9 us -> 41.2 us  [padded(): lax.ppermute(lax.slice_in_dim(block, block.shape[dim] - width, None, axis...]
    dot_general x2, matrix products: 10.9 us -> 24.3 us  [on_device(): jnp.dot(coarse_inverse, jnp.concatenate(lax.all_to_all(jnp.stack([group_b...]
    another operation x1 -> x3, local copies, waits for them, and re-layouts: 0.01 us -> 6.62 us  [the longest x2 6.61 us: on_device(): jnp.stack([group_block] * lax.axis_size('grp'))]
    all_gather x2, blocking collectives: 78.8 us -> 73.5 us  [on_device(): group_block = lax.all_gather(restricted, 'mem', axis=0, tiled=True)]
  transfers between devices with their start and end apart: 22 -> 22, of which waited for: 10 -> 10; matrix products, arithmetic and copies ran while one was open for 7% -> 5% of each run, Pallas kernels for 0% -> 0%
where the time goes in v1:
time: 414 us; the launch traced here: 407 us
  waiting for transfers between devices  161 us (39%)
  starting transfers between devices  103 us (25%)
  blocking collectives  73.5 us (18%)
  matrix products  40.6 us (10%)
  local copies, waits for them, and re-layouts  16.2 us (4%)
  other arithmetic  12.1 us (3%)
    ppermute x10, waiting for transfers between devices, padded(): lax.ppermute(lax.slice_in_dim(block, block.shape[dim] - width, None, axis...  126 us
    all_gather x2, blocking collectives, on_device(): group_block = lax.all_gather(restricted, 'mem', axis=0, tiled=True)  73.5 us
    ppermute x10, starting transfers between devices, padded(): lax.ppermute(lax.slice_in_dim(block, block.shape[dim] - width, None, axis...  41.2 us
    all_to_all x2, starting transfers between devices, on_device(): lax.all_to_all(jnp.stack([group_block] * lax.axis_size('grp')), 'grp', 0, 0)  36.5 us
    ppermute x10, waiting for transfers between devices, padded(): lax.ppermute(lax.slice_in_dim(block, 0, width, axis=dim), axis, backward)  34.6 us
    ppermute x10, starting transfers between devices, padded(): lax.ppermute(lax.slice_in_dim(block, 0, width, axis=dim), axis, backward)  25.2 us
    dot_general x2, matrix products, on_device(): jnp.dot(coarse_inverse, jnp.concatenate(lax.all_to_all(jnp.stack([group_b...  24.3 us
    dot_general x2, matrix products, on_device(): jnp.dot(owned_inverse, flat_rows, preferred_element_type=jnp.float32)  10 us
  transfers between devices with their start and end apart: 22, of which 10 were waited for; matrix products, arithmetic and copies ran while one was open for 5% of the time, Pallas kernels for 0%

profile of v1, /device:TPU:65, one launch (start us, length us, event | category | flops | bytes accessed | tf_op | source)
XLA Modules:
  0.0 406.8 jit_solution(237056628770910882)
XLA Ops:
  0.8 2.6 collective-permute-start
  3.3 3.0 collective-permute-start.2
  8.3 3.6 collective-permute-start.3
  14.7 6.2 %collective-permute-start.6 = (f32[26,1]{1,0:T(8,128)S(1)}, f32[26,1]{1,0:T(8,128)S(1)}, u32[]{:S(2)}, u32[]{:S(2)}) collective-permute-start(f32[26,1]{1,0:T(8,128)S(1)} %get-tuple-element.24), channel_id=1, source_target_pairs={{0,1},{1,2},{2,3},{3,4},{4,5},{5,6},{6,7},{7,8},{8,9},{9,10},{10,1... | collective-permute-start | bytes 320 | tf_op jit(solution)/shard_map/ppermute | solution.py:15
  23.1 5.5 %collective-permute-start.7 = (f32[26,1,384]{2,1,0:T(1,128)S(1)}, f32[26,1,384]{2,1,0:T(1,128)S(1)}, u32[]{:S(2)}, u32[]{:S(2)}) collective-permute-start(f32[26,1,384]{2,1,0:T(1,128)S(1)} %get-tuple-element.12), channel_id=1, source_target_pairs={{0,1},{1,2},{2,3},{3,4},{4,5},{5,6},{6,7},{7,8},{8,9},{9,10},{10,1... | collective-permute-start | bytes 119816 | tf_op jit(solution)/shard_map/ppermute | solution.py:15
  29.7 3.1 fusion.34
  34.1 38.8 %all_gather.6 = f32[256,384]{1,0:T(8,128)S(1)} all-gather(f32[16,384]{1,0:T(8,128)S(1)} %convolution_bitcast_fusion.1), channel_id=1, replica_groups=mesh['grp'=16,'mem'=16] {'mem'}, dimensions={0}, use_global_device_ids=true | all-gather | bytes 417792 | tf_op jit(solution)/shard_map/all_gather | solution.py:73
  73.0 3.3 stack.4
  76.3 13.5 %all-to-all-start = ((f32[16,256,384]{2,1,0:T(8,128)}), f32[16,256,384]{2,1,0:T(8,128)}, u32[]{:S(2)}, u32[]{:S(2)}) async-start(f32[16,256,384]{2,1,0:T(8,128)} %stack.4), calls=%async_computation | async-start | bytes 12582912 | tf_op jit(solution)/shard_map/all_to_all | solution.py:77
  89.8 3.5 collective-permute-start.8
  95.3 49.1 %collective-permute-done.8 = bf16[4,56,384]{2,1,0:T(8,128)(2,1)S(1)} collective-permute-done((bf16[4,56,384]{2,1,0:T(8,128)(2,1)S(1)}, bf16[4,56,384]{2,1,0:T(8,128)(2,1)S(1)}, u32[]{:S(2)}, u32[]{:S(2)}) %collective-permute-start.8) | collective-permute-done | bytes 172064 | tf_op jit(solution)/shard_map/ppermute | solution.py:15
  144.4 17.2 %collective-permute-done.9 = bf16[4,56,384]{2,1,0:T(8,128)(2,1)S(1)} collective-permute-done((bf16[4,56,384]{2,1,0:T(8,128)(2,1)S(1)}, bf16[4,56,384]{2,1,0:T(8,128)(2,1)S(1)}, u32[]{:S(2)}, u32[]{:S(2)}) %collective-permute-start.9) | collective-permute-done | bytes 172064 | tf_op jit(solution)/shard_map/ppermute | solution.py:18
  163.6 4.3 %collective-permute-start.11 = (bf16[32,4,384]{2,1,0:T(4,128)(2,1)S(1)}, bf16[32,4,384]{2,1,0:T(4,128)(2,1)S(1)}, u32[]{:S(2)}, u32[]{:S(2)}) collective-permute-start(bf16[32,4,384]{2,1,0:T(4,128)(2,1)S(1)} %get-tuple-element.18), channel_id=1, source_target_pairs={{1,0},{2,1},{3,2},{4,3},{5,4},{6,5},{7,6},{8,7},{9,8},{10,9},{11,1... | collective-permute-start | bytes 294920 | tf_op jit(solution)/shard_map/ppermute | solution.py:18
  168.1 8.3 %slice.148 = bf16[24,56,2048]{2,1,0:T(8,128)(2,1)} slice(bf16[32,64,2048]{2,1,0:T(8,128)(2,1)} %bitcast.52), slice={[4:28], [4:60], [0:2048]} | slice | bytes 11010048 | tf_op jit(solution)/shard_map/slice | solution.py:50
  176.4 8.5 %collective-permute-done.10 = bf16[32,4,384]{2,1,0:T(4,128)(2,1)S(1)} collective-permute-done((bf16[32,4,384]{2,1,0:T(4,128)(2,1)S(1)}, bf16[32,4,384]{2,1,0:T(4,128)(2,1)S(1)}, u32[]{:S(2)}, u32[]{:S(2)}) %collective-permute-start.10) | collective-permute-done | bytes 98336 | tf_op jit(solution)/shard_map/ppermute | solution.py:15
  184.9 2.1 pad_maximum_fusion.14
  186.9 12.3 %fusion.40 = f32[384,16]{1,0:T(8,128)S(1)} fusion(f32[4096,384]{1,0:T(8,128)} %bitcast.5, f32[16,4096]{1,0:T(8,128)S(1)} %copy-done), kind=kOutput, calls=%fused_computation.83 | convolution fusion | flops 301989888 | bytes 6578176 | tf_op jit(solution)/shard_map/dot_general | solution.py:74
  201.2 3.1 convolution_add_fusion
  204.4 2.6 collective-permute-start.12
  207.0 6.3 %collective-permute-start.13 = (f32[1,56,384]{2,1,0:T(8,128)S(1)}, f32[1,56,384]{2,1,0:T(8,128)S(1)}, u32[]{:S(2)}, u32[]{:S(2)}) collective-permute-start(f32[1,56,384]{2,1,0:T(8,128)S(1)} %get-tuple-element.13), channel_id=1, source_target_pairs={{0,16},{16,32},{32,48},{48,64},{64,80},{80,96},{96,112},{112,128},... | collective-permute-start | bytes 258056 | tf_op jit(solution)/shard_map/ppermute | solution.py:15
  216.9 5.5 %collective-permute-start.15 = (f32[26,1,384]{2,1,0:T(1,128)S(1)}, f32[26,1,384]{2,1,0:T(1,128)S(1)}, u32[]{:S(2)}, u32[]{:S(2)}) collective-permute-start(f32[26,1,384]{2,1,0:T(1,128)S(1)} %get-tuple-element.10), channel_id=1, source_target_pairs={{0,1},{1,2},{2,3},{3,4},{4,5},{5,6},{6,7},{7,8},{8,9},{9,10},{10,1... | collective-permute-start | bytes 119816 | tf_op jit(solution)/shard_map/ppermute | solution.py:15
  223.5 3.4 fusion.32
  228.2 34.6 %all_gather.7 = f32[256,384]{1,0:T(8,128)S(1)} all-gather(f32[16,384]{1,0:T(8,128)S(1)} %convolution_bitcast_fusion), channel_id=1, replica_groups=mesh['grp'=16,'mem'=16] {'mem'}, dimensions={0}, use_global_device_ids=true | all-gather | bytes 417792 | tf_op jit(solution)/shard_map/all_gather | solution.py:73
  262.8 3.3 stack.5
  266.1 23.0 %all-to-all-start.1 = ((f32[16,256,384]{2,1,0:T(8,128)}), f32[16,256,384]{2,1,0:T(8,128)}, u32[]{:S(2)}, u32[]{:S(2)}) async-start(f32[16,256,384]{2,1,0:T(8,128)} %stack.5), calls=%async_computation.1 | async-start | bytes 12582912 | tf_op jit(solution)/shard_map/all_to_all | solution.py:77
  289.1 3.5 collective-permute-start.16
  294.6 49.1 %collective-permute-done.16 = bf16[4,56,384]{2,1,0:T(8,128)(2,1)S(1)} collective-permute-done((bf16[4,56,384]{2,1,0:T(8,128)(2,1)S(1)}, bf16[4,56,384]{2,1,0:T(8,128)(2,1)S(1)}, u32[]{:S(2)}, u32[]{:S(2)}) %collective-permute-start.16) | collective-permute-done | bytes 172064 | tf_op jit(solution)/shard_map/ppermute | solution.py:15
  343.7 17.2 %collective-permute-done.17 = bf16[4,56,384]{2,1,0:T(8,128)(2,1)S(1)} collective-permute-done((bf16[4,56,384]{2,1,0:T(8,128)(2,1)S(1)}, bf16[4,56,384]{2,1,0:T(8,128)(2,1)S(1)}, u32[]{:S(2)}, u32[]{:S(2)}) %collective-permute-start.17) | collective-permute-done | bytes 172064 | tf_op jit(solution)/shard_map/ppermute | solution.py:18
  363.0 4.2 %collective-permute-start.19 = (bf16[32,4,384]{2,1,0:T(4,128)(2,1)S(1)}, bf16[32,4,384]{2,1,0:T(4,128)(2,1)S(1)}, u32[]{:S(2)}, u32[]{:S(2)}) collective-permute-start(bf16[32,4,384]{2,1,0:T(4,128)(2,1)S(1)} %get-tuple-element.16), channel_id=1, source_target_pairs={{1,0},{2,1},{3,2},{4,3},{5,4},{6,5},{7,6},{8,7},{9,8},{10,9},{11,1... | collective-permute-start | bytes 294920 | tf_op jit(solution)/shard_map/ppermute | solution.py:18
  367.2 16.3 %collective-permute-done.18 = bf16[32,4,384]{2,1,0:T(4,128)(2,1)S(1)} collective-permute-done((bf16[32,4,384]{2,1,0:T(4,128)(2,1)S(1)}, bf16[32,4,384]{2,1,0:T(4,128)(2,1)S(1)}, u32[]{:S(2)}, u32[]{:S(2)}) %collective-permute-start.18) | collective-permute-done | bytes 98336 | tf_op jit(solution)/shard_map/ppermute | solution.py:15
  384.4 6.9 %fusion.44 = f32[384,1344]{0,1:T(8,128)} fusion(bf16[1344,2048]{1,0:T(8,128)(2,1)} %bitcast.50, bf16[2048,384]{1,0:T(8,128)(2,1)S(1)} %bitcast.55), kind=kOutput, calls=%fused_computation.87 | convolution fusion | flops 2113929216 | bytes 9142272 | tf_op jit(solution)/shard_map/dot_general | solution.py:63
  391.3 12.0 %fusion.42 = f32[384,16]{1,0:T(8,128)S(1)} fusion(f32[4096,384]{1,0:T(8,128)} %bitcast.16, f32[16,4096]{1,0:T(8,128)S(1)} %copy-done), kind=kOutput, calls=%fused_computation.85 | convolution fusion | flops 301989888 | bytes 6578176 | tf_op jit(solution)/shard_map/dot_general | solution.py:74
  (81 shorter events, 30.1 us)
Async XLA Ops:
  0.0 186.9 %copy-start = (f32[16,4096]{1,0:T(8,128)S(1)}, f32[16,4096]{1,0:T(8,128)}, u32[]{:S(2)}) copy-start(f32[16,4096]{1,0:T(8,128)} %param.9) | copy-start | bytes 786436
  0.8 11.2 %collective-permute-start = (f32[1,56]{1,0:T(1,128)S(1)}, f32[1,56]{1,0:T(1,128)S(1)}, u32[]{:S(2)}, u32[]{:S(2)}) collective-permute-start(f32[1,56]{1,0:T(1,128)S(1)} %get-tuple-element.30), channel_id=1, source_target_pairs={{16,0},{32,16},{48,32},{64,48},{80,64},{96,80},{112,96},{128,112},... | collective-permute-start | bytes 680 | tf_op jit(solution)/shard_map/ppermute | solution.py:18
  3.3 8.6 %collective-permute-start.2 = (f32[1,56]{1,0:T(1,128)S(1)}, f32[1,56]{1,0:T(1,128)S(1)}, u32[]{:S(2)}, u32[]{:S(2)}) collective-permute-start(f32[1,56]{1,0:T(1,128)S(1)} %get-tuple-element.29), channel_id=1, source_target_pairs={{0,16},{16,32},{32,48},{48,64},{64,80},{80,96},{96,112},{112,128},... | collective-permute-start | bytes 680 | tf_op jit(solution)/shard_map/ppermute | solution.py:15
  6.4 14.6 %collective-permute-start.1 = (f32[1,56,384]{2,1,0:T(8,128)S(1)}, f32[1,56,384]{2,1,0:T(8,128)S(1)}, u32[]{:S(2)}, u32[]{:S(2)}) collective-permute-start(f32[1,56,384]{2,1,0:T(8,128)S(1)} %broadcast.19), channel_id=1, source_target_pairs={{16,0},{32,16},{48,32},{64,48},{80,64},{96,80},{112,96},{128,112},... | collective-permute-start | bytes 258056 | tf_op jit(solution)/shard_map/ppermute | solution.py:18
  8.3 12.7 %collective-permute-start.3 = (f32[1,56,384]{2,1,0:T(8,128)S(1)}, f32[1,56,384]{2,1,0:T(8,128)S(1)}, u32[]{:S(2)}, u32[]{:S(2)}) collective-permute-start(f32[1,56,384]{2,1,0:T(8,128)S(1)} %broadcast.19), channel_id=1, source_target_pairs={{0,16},{16,32},{32,48},{48,64},{64,80},{80,96},{96,112},{112,128},... | collective-permute-start | bytes 258056 | tf_op jit(solution)/shard_map/ppermute | solution.py:15
  12.8 15.8 %collective-permute-start.4 = (f32[26,1]{1,0:T(8,128)S(1)}, f32[26,1]{1,0:T(8,128)S(1)}, u32[]{:S(2)}, u32[]{:S(2)}) collective-permute-start(f32[26,1]{1,0:T(8,128)S(1)} %get-tuple-element.23), channel_id=1, source_target_pairs={{1,0},{2,1},{3,2},{4,3},{5,4},{6,5},{7,6},{8,7},{9,8},{10,9},{11,1... | collective-permute-start | bytes 320 | tf_op jit(solution)/shard_map/ppermute | solution.py:18
  14.7 13.9 %copy-start.17 = (f32[24,56]{1,0:T(8,128)S(1)}, f32[24,56]{1,0:T(8,128)}, u32[]{:S(2)}) copy-start(f32[24,56]{1,0:T(8,128)} %param.6) | copy-start | bytes 16132
  14.7 15.0 %copy-start.1 = (f32[24,56,384]{2,1,0:T(8,128)S(1)}, f32[24,56,384]{2,1,0:T(8,128)}, u32[]{:S(2)}) copy-start(f32[24,56,384]{2,1,0:T(8,128)} %param.5) | copy-start | bytes 6193156
  14.7 13.9 %collective-permute-start.6 = (f32[26,1]{1,0:T(8,128)S(1)}, f32[26,1]{1,0:T(8,128)S(1)}, u32[]{:S(2)}, u32[]{:S(2)}) collective-permute-start(f32[26,1]{1,0:T(8,128)S(1)} %get-tuple-element.24), channel_id=1, source_target_pairs={{0,1},{1,2},{2,3},{3,4},{4,5},{5,6},{6,7},{7,8},{8,9},{9,10},{10,1... | collective-permute-start | bytes 320 | tf_op jit(solution)/shard_map/ppermute | solution.py:15
  21.2 7.6 %collective-permute-start.5 = (f32[26,1,384]{2,1,0:T(1,128)S(1)}, f32[26,1,384]{2,1,0:T(1,128)S(1)}, u32[]{:S(2)}, u32[]{:S(2)}) collective-permute-start(f32[26,1,384]{2,1,0:T(1,128)S(1)} %get-tuple-element.11), channel_id=1, source_target_pairs={{1,0},{2,1},{3,2},{4,3},{5,4},{6,5},{7,6},{8,7},{9,8},{10,9},{11,1... | collective-permute-start | bytes 119816 | tf_op jit(solution)/shard_map/ppermute | solution.py:18
  23.1 6.6 %collective-permute-start.7 = (f32[26,1,384]{2,1,0:T(1,128)S(1)}, f32[26,1,384]{2,1,0:T(1,128)S(1)}, u32[]{:S(2)}, u32[]{:S(2)}) collective-permute-start(f32[26,1,384]{2,1,0:T(1,128)S(1)} %get-tuple-element.12), channel_id=1, source_target_pairs={{0,1},{1,2},{2,3},{3,4},{4,5},{5,6},{6,7},{7,8},{8,9},{9,10},{10,1... | collective-permute-start | bytes 119816 | tf_op jit(solution)/shard_map/ppermute | solution.py:15
  76.3 110.7 %all-to-all-start = ((f32[16,256,384]{2,1,0:T(8,128)}), f32[16,256,384]{2,1,0:T(8,128)}, u32[]{:S(2)}, u32[]{:S(2)}) async-start(f32[16,256,384]{2,1,0:T(8,128)} %stack.4), calls=%async_computation | async-start | bytes 12582912 | tf_op jit(solution)/shard_map/all_to_all | solution.py:77
  89.8 54.6 %collective-permute-start.8 = (bf16[4,56,384]{2,1,0:T(8,128)(2,1)S(1)}, bf16[4,56,384]{2,1,0:T(8,128)(2,1)S(1)}, u32[]{:S(2)}, u32[]{:S(2)}) collective-permute-start(bf16[4,56,384]{2,1,0:T(8,128)(2,1)S(1)} %get-tuple-element.21), channel_id=1, source_target_pairs={{0,16},{16,32},{32,48},{48,64},{64,80},{80,96},{96,112},{112,128},... | collective-permute-start | bytes 516104 | tf_op jit(solution)/shard_map/ppermute | solution.py:15
  93.4 68.2 %collective-permute-start.9 = (bf16[4,56,384]{2,1,0:T(8,128)(2,1)S(1)}, bf16[4,56,384]{2,1,0:T(8,128)(2,1)S(1)}, u32[]{:S(2)}, u32[]{:S(2)}) collective-permute-start(bf16[4,56,384]{2,1,0:T(8,128)(2,1)S(1)} %get-tuple-element.22), channel_id=1, source_target_pairs={{16,0},{32,16},{48,32},{64,48},{80,64},{96,80},{112,96},{128,112},... | collective-permute-start | bytes 516104 | tf_op jit(solution)/shard_map/ppermute | solution.py:18
  161.7 23.2 %collective-permute-start.10 = (bf16[32,4,384]{2,1,0:T(4,128)(2,1)S(1)}, bf16[32,4,384]{2,1,0:T(4,128)(2,1)S(1)}, u32[]{:S(2)}, u32[]{:S(2)}) collective-permute-start(bf16[32,4,384]{2,1,0:T(4,128)(2,1)S(1)} %get-tuple-element.17), channel_id=1, source_target_pairs={{0,1},{1,2},{2,3},{3,4},{4,5},{5,6},{6,7},{7,8},{8,9},{9,10},{10,1... | collective-permute-start | bytes 294920 | tf_op jit(solution)/shard_map/ppermute | solution.py:15
  163.6 21.2 %collective-permute-start.11 = (bf16[32,4,384]{2,1,0:T(4,128)(2,1)S(1)}, bf16[32,4,384]{2,1,0:T(4,128)(2,1)S(1)}, u32[]{:S(2)}, u32[]{:S(2)}) collective-permute-start(bf16[32,4,384]{2,1,0:T(4,128)(2,1)S(1)} %get-tuple-element.18), channel_id=1, source_target_pairs={{1,0},{2,1},{3,2},{4,3},{5,4},{6,5},{7,6},{8,7},{9,8},{10,9},{11,1... | collective-permute-start | bytes 294920 | tf_op jit(solution)/shard_map/ppermute | solution.py:18
  168.1 31.2 %copy-start.7 = (f32[1344,16]{0,1:T(8,128)}, f32[1344,16]{0,1:T(8,128)S(1)}, u32[]{:S(2)}) copy-start(f32[1344,16]{0,1:T(8,128)S(1)} %reshape.46) | copy-start | bytes 258052
  186.9 14.2 %copy-start.3 = (bf16[24,56,2048]{2,1,0:T(8,128)(2,1)S(1)}, bf16[24,56,2048]{2,1,0:T(8,128)(2,1)}, u32[]{:S(2)}) copy-start(bf16[24,56,2048]{2,1,0:T(8,128)(2,1)} %slice.148) | copy-start | bytes 16515076
  204.3 19.1 %copy-start.2 = (f32[24,56,384]{2,1,0:T(8,128)S(1)}, f32[24,56,384]{2,1,0:T(8,128)}, u32[]{:S(2)}) copy-start(f32[24,56,384]{2,1,0:T(8,128)} %param.5) | copy-start | bytes 6193156
  204.4 19.1 %copy-start.10 = (f32[24,56]{1,0:T(8,128)S(1)}, f32[24,56]{1,0:T(8,128)}, u32[]{:S(2)}) copy-start(f32[24,56]{1,0:T(8,128)} %copy-done.9) | copy-start | bytes 16132
  204.4 19.1 %copy-start.12 = (f32[24,56]{1,0:T(8,128)S(1)}, f32[24,56]{1,0:T(8,128)}, u32[]{:S(2)}) copy-start(f32[24,56]{1,0:T(8,128)} %copy-done.11) | copy-start | bytes 16132
  204.4 19.1 %copy-start.14 = (f32[24,56]{1,0:T(8,128)S(1)}, f32[24,56]{1,0:T(8,128)}, u32[]{:S(2)}) copy-start(f32[24,56]{1,0:T(8,128)} %copy-done.13) | copy-start | bytes 16132
  204.4 19.1 %copy-start.16 = (f32[24,56]{1,0:T(8,128)S(1)}, f32[24,56]{1,0:T(8,128)}, u32[]{:S(2)}) copy-start(f32[24,56]{1,0:T(8,128)} %copy-done.15) | copy-start | bytes 16132
  204.4 9.2 %collective-permute-start.12 = (f32[1,56,384]{2,1,0:T(8,128)S(1)}, f32[1,56,384]{2,1,0:T(8,128)S(1)}, u32[]{:S(2)}, u32[]{:S(2)}) collective-permute-start(f32[1,56,384]{2,1,0:T(8,128)S(1)} %get-tuple-element.14), channel_id=1, source_target_pairs={{16,0},{32,16},{48,32},{64,48},{80,64},{96,80},{112,96},{128,112},... | collective-permute-start | bytes 258056 | tf_op jit(solution)/shard_map/ppermute | solution.py:18
  207.0 7.9 %collective-permute-start.13 = (f32[1,56,384]{2,1,0:T(8,128)S(1)}, f32[1,56,384]{2,1,0:T(8,128)S(1)}, u32[]{:S(2)}, u32[]{:S(2)}) collective-permute-start(f32[1,56,384]{2,1,0:T(8,128)S(1)} %get-tuple-element.13), channel_id=1, source_target_pairs={{0,16},{16,32},{32,48},{48,64},{64,80},{80,96},{96,112},{112,128},... | collective-permute-start | bytes 258056 | tf_op jit(solution)/shard_map/ppermute | solution.py:15
  215.0 7.4 %collective-permute-start.14 = (f32[26,1,384]{2,1,0:T(1,128)S(1)}, f32[26,1,384]{2,1,0:T(1,128)S(1)}, u32[]{:S(2)}, u32[]{:S(2)}) collective-permute-start(f32[26,1,384]{2,1,0:T(1,128)S(1)} %get-tuple-element.9), channel_id=1, source_target_pairs={{1,0},{2,1},{3,2},{4,3},{5,4},{6,5},{7,6},{8,7},{9,8},{10,9},{11,1... | collective-permute-start | bytes 119816 | tf_op jit(solution)/shard_map/ppermute | solution.py:18
  216.9 6.5 %collective-permute-start.15 = (f32[26,1,384]{2,1,0:T(1,128)S(1)}, f32[26,1,384]{2,1,0:T(1,128)S(1)}, u32[]{:S(2)}, u32[]{:S(2)}) collective-permute-start(f32[26,1,384]{2,1,0:T(1,128)S(1)} %get-tuple-element.10), channel_id=1, source_target_pairs={{0,1},{1,2},{2,3},{3,4},{4,5},{5,6},{6,7},{7,8},{8,9},{9,10},{10,1... | collective-permute-start | bytes 119816 | tf_op jit(solution)/shard_map/ppermute | solution.py:15
  266.1 125.2 %all-to-all-start.1 = ((f32[16,256,384]{2,1,0:T(8,128)}), f32[16,256,384]{2,1,0:T(8,128)}, u32[]{:S(2)}, u32[]{:S(2)}) async-start(f32[16,256,384]{2,1,0:T(8,128)} %stack.5), calls=%async_computation.1 | async-start | bytes 12582912 | tf_op jit(solution)/shard_map/all_to_all | solution.py:77
  289.1 54.6 %collective-permute-start.16 = (bf16[4,56,384]{2,1,0:T(8,128)(2,1)S(1)}, bf16[4,56,384]{2,1,0:T(8,128)(2,1)S(1)}, u32[]{:S(2)}, u32[]{:S(2)}) collective-permute-start(bf16[4,56,384]{2,1,0:T(8,128)(2,1)S(1)} %get-tuple-element.19), channel_id=1, source_target_pairs={{0,16},{16,32},{32,48},{48,64},{64,80},{80,96},{96,112},{112,128},... | collective-permute-start | bytes 516104 | tf_op jit(solution)/shard_map/ppermute | solution.py:15
  292.7 68.2 %collective-permute-start.17 = (bf16[4,56,384]{2,1,0:T(8,128)(2,1)S(1)}, bf16[4,56,384]{2,1,0:T(8,128)(2,1)S(1)}, u32[]{:S(2)}, u32[]{:S(2)}) collective-permute-start(bf16[4,56,384]{2,1,0:T(8,128)(2,1)S(1)} %get-tuple-element.20), channel_id=1, source_target_pairs={{16,0},{32,16},{48,32},{64,48},{80,64},{96,80},{112,96},{128,112},... | collective-permute-start | bytes 516104 | tf_op jit(solution)/shard_map/ppermute | solution.py:18
  361.0 22.5 %collective-permute-start.18 = (bf16[32,4,384]{2,1,0:T(4,128)(2,1)S(1)}, bf16[32,4,384]{2,1,0:T(4,128)(2,1)S(1)}, u32[]{:S(2)}, u32[]{:S(2)}) collective-permute-start(bf16[32,4,384]{2,1,0:T(4,128)(2,1)S(1)} %get-tuple-element.15), channel_id=1, source_target_pairs={{0,1},{1,2},{2,3},{3,4},{4,5},{5,6},{6,7},{7,8},{8,9},{9,10},{10,1... | collective-permute-start | bytes 294920 | tf_op jit(solution)/shard_map/ppermute | solution.py:15
  363.0 20.5 %collective-permute-start.19 = (bf16[32,4,384]{2,1,0:T(4,128)(2,1)S(1)}, bf16[32,4,384]{2,1,0:T(4,128)(2,1)S(1)}, u32[]{:S(2)}, u32[]{:S(2)}) collective-permute-start(bf16[32,4,384]{2,1,0:T(4,128)(2,1)S(1)} %get-tuple-element.16), channel_id=1, source_target_pairs={{1,0},{2,1},{3,2},{4,3},{5,4},{6,5},{7,6},{8,7},{9,8},{10,9},{11,1... | collective-permute-start | bytes 294920 | tf_op jit(solution)/shard_map/ppermute | solution.py:18
  (8 other events, 35.2 us)
